TPU v7x, 128 devices: a whole 4x4x4 slice. The times are simulated.
128 devices in a mesh: dp: 16 (over x, y), cent: 8 (over z, core).
Axes of the slice: x: 4, y: 4, z: 4, core: 2. Of those that a mesh axis runs over, the one named last changes fastest.
Arguments:
- embeddings: bfloat16 [65536, 1024], P('dp'), may hold values from -2000 to 2000
- centroids: bfloat16 [16384, 1024], P('cent'), may hold values from -2000 to 2000
- kmeans_id: int32 [65536], P('dp'), may hold values from 0 to 16383, as said below
- members: int32 [512, 16, 16], P(None, 'dp'), may hold values from 0 to 4095, as said below
- counts: int32 [512, 16], P(None, 'dp'), may hold values from 4 to 16, as said below
- owner_groups: int32 [16, 8, 4], replicated, may hold values from 0 to 511, as said below
Outputs:
- best_score: float32 [65536], P('dp')
- new_centroids: float32 [1024, 16384], P('dp', 'cent')
- slot_max: float32 [16, 8, 4, 256], P('dp', 'cent')
Inputs may be any that keep to these rules, and one draw needn't show every extreme that they name: `kmeans_id`: for each index of dp, exactly 512 of its 4096 rows have an id in each aligned block of 2048 centroids. `members`: entries past counts[g, s] are 0; the valid entries of all clusters for one index s of dp list each of its 4096 local rows exactly once. For each index of dp the counts sum to 4096; some cluster has 16 valid entries from every index of dp. `owner_groups`: every cluster appears exactly once.
All inputs are finite; a program needn't handle non-finite values.
Results may differ from a plain program's by a relative error of at most 0.0021.
Values may be sent and summed in bfloat16 or wider, within the bound.
A program may use at most 128 MiB of HBM per device.

v0:
```python
import jax
import jax.numpy as jnp
from jax import lax
from jax.sharding import PartitionSpec as P

epsilon = 1e-06


def normalize_rows(values):
    wide = values.astype(jnp.float32)
    return (wide / jnp.sqrt(jnp.sum(wide * wide, axis=1, keepdims=True) + epsilon)).astype(
        jnp.bfloat16
    )


def shards(embeddings, centroids, kmeans_id, members, counts, owner_groups):
    row_count, feat_width = embeddings.shape
    cent_shard = centroids.shape[0]
    dp_count = lax.axis_size("dp")
    cent_count = lax.axis_size("cent")
    feat_part = feat_width // dp_count
    share_rows = row_count // cent_count
    cent_index = lax.axis_index("cent")
    dp_index = lax.axis_index("dp")
    unit_rows = normalize_rows(embeddings)
    cent_units = normalize_rows(centroids)
    block_rows = min(512, row_count)

    def block_best(portion):
        scores = lax.dot_general(
            portion, cent_units, (((1,), (1,)), ((), ())), preferred_element_type=jnp.float32
        )
        return jnp.max(scores, axis=1)

    local_best = lax.map(
        block_best, unit_rows.reshape(row_count // block_rows, block_rows, feat_width)
    ).reshape(row_count)
    best_score = lax.pmax(local_best, "cent")
    cent_columns = jnp.arange(cent_shard, dtype=jnp.int32)
    in_shard = kmeans_id // cent_shard == cent_index
    chosen = jnp.nonzero(in_shard, size=share_rows, fill_value=0)[0].astype(jnp.int32)
    chosen_rows = unit_rows[chosen]
    chosen_ids = kmeans_id[chosen] - cent_index * cent_shard
    onehot_table = (chosen_ids[:, None] == cent_columns[None, :]).astype(jnp.bfloat16)
    partial_sums = lax.dot_general(
        onehot_table, chosen_rows, (((0,), (0,)), ((), ())), preferred_element_type=jnp.float32
    )
    summed = lax.psum(partial_sums, "dp")
    scaled = summed / jnp.maximum(jnp.sqrt(jnp.sum(summed * summed, axis=1, keepdims=True)), 1.0)
    new_part = jnp.transpose(lax.dynamic_slice_in_dim(scaled, dp_index * feat_part, feat_part, 1))
    sub_slots = members.shape[2]
    own_count = owner_groups.shape[2]
    owned_here = lax.dynamic_index_in_dim(owner_groups, cent_index, 1, keepdims=False)
    local_members = members[:, 0, :]
    local_counts = counts[:, 0]
    picked = local_members[owned_here]
    sent_rows = unit_rows[picked]
    slot_ids = jnp.arange(sub_slots, dtype=jnp.int32)
    sent_live = (slot_ids[None, None, :] < local_counts[owned_here][:, :, None]).astype(
        jnp.bfloat16
    )
    cluster_rows = lax.all_to_all(sent_rows, "dp", split_axis=0, concat_axis=0, tiled=True)
    live_marks = lax.all_to_all(sent_live, "dp", split_axis=0, concat_axis=0, tiled=True)
    item_count = cluster_rows.shape[1]
    block_span = cluster_rows.shape[0] * sub_slots
    similarity = jnp.einsum(
        "sgqd,tgpd->gsqtp", cluster_rows, cluster_rows, preferred_element_type=jnp.float32
    )
    similarity = similarity.reshape(item_count, block_span, block_span)
    live_flags = jnp.transpose(live_marks, (1, 0, 2)).reshape(item_count, block_span) > 0.5
    diagonal = jnp.arange(block_span)[:, None] == jnp.arange(block_span)[None, :]
    usable = live_flags[:, :, None] & live_flags[:, None, :] & jnp.logical_not(diagonal)[None]
    largest = jnp.max(jnp.where(usable, similarity, -jnp.inf), axis=2)
    slot_values = jnp.where(jnp.any(usable, axis=2), largest, -1.0)
    slot_max = slot_values.reshape(1, 1, own_count, dp_count * sub_slots)
    return (best_score, new_part, slot_max)


def solution(mesh):
    placed = (P("dp", None), P("cent", None), P("dp"), P(None, "dp", None), P(None, "dp"), P())
    return jax.shard_map(
        shards,
        mesh=mesh,
        in_specs=placed,
        out_specs=(P("dp"), P("dp", "cent"), P("dp", "cent", None, None)),
        check_vma=False,
    )
```

profile of v0, /device:TPU:1, one launch (start us, length us, event | category | flops | bytes accessed | tf_op | source)
XLA Modules:
  0.0 259.5 jit_solution(2537292319106814998)
XLA Ops:
  7.2 0.0 copy-start
  7.2 0.7 compare_select_fusion.6
  7.9 0.1 copy.33
  8.0 0.1 reshape.275
  8.1 0.8 gather_fusion.2
  8.9 0.1 reshape.274
  9.0 0.7 fusion.13
  9.7 7.6 %all-to-all-start = ((bf16[16,4,16]{2,1,0:T(4,128)(2,1)}), bf16[16,4,16]{2,1,0:T(4,128)(2,1)S(1)}, u32[]{:S(2)}, u32[]{:S(2)}) async-start(bf16[16,4,16]{2,1,0:T(4,128)(2,1)} %fusion.13), calls=%async_computation | async-start | bytes 32768 | tf_op jit(solution)/shard_map/all_to_all | solution.py:63
  17.3 0.0 all-reduce.2.cloned.1.call-start
  17.3 0.6 convert_reduce_fusion
  18.0 0.3 reduce-window.16
  18.3 0.1 slice.28
  18.3 0.1 reduce-window.19
  18.4 0.1 slice_reduce_fusion
  18.5 0.1 broadcast_add_fusion
  18.6 5.1 %fusion.3 = f32[4096]{0:T(1024)S(1)} fusion(bf16[4096,1024]{1,0:T(8,128)(2,1)} %param.8), kind=kLoop, calls=%fused_computation.12 | loop fusion | flops 12578816 | bytes 8404992 | tf_op jit(solution)/shard_map/reduce_sum | solution.py:11
  23.7 29.0 %scatter_custom_fusion = s32[512]{0:T(512)S(1)} fusion(s32[4096]{0:T(1024)S(1)} %bitcast.53, s32[4096]{0:T(1024)S(1)} %ne.48, s32[]{:T(128)} %constant.56.clone.1), kind=kCustom, calls=%fused_computation.66 | custom fusion | flops 4096 | bytes 2052 | tf_op jit(solution)/shard_map/scatter-add | solution.py:41
  52.7 0.3 reduce-window.24
  53.0 0.1 slice.16
  53.1 0.1 slice_reduce_fusion.1
  53.2 0.1 broadcast_add_fusion.1
  53.3 0.7 compare_select_fusion.2
  54.0 3.1 %gather_fusion = s32[512]{0:T(512)S(1)} fusion(s32[4096]{0:T(1024)S(1)} %copy-done.1, s32[1024]{0:T(1024)S(1)} %pad_clamp_fusion.1), kind=kCustom, calls=%fused_computation | custom fusion | bytes 6144 | tf_op jit(solution)/shard_map/gather | solution.py:43
  57.1 8.5 %fusion.4 = bf16[4096,1024]{1,0:T(8,128)(2,1)} fusion(bf16[4096,1024]{1,0:T(8,128)(2,1)} %param.8, f32[4096]{0:T(1024)S(1)} %add_sqrt_fusion), kind=kLoop, calls=%fused_computation.13 | loop fusion | flops 12582912 | bytes 16793600 | tf_op jit(solution)/shard_map/convert_element_type | solution.py:11
  65.6 7.2 %gather_fusion.1 = bf16[512,1024]{1,0:T(8,128)(2,1)S(1)} fusion(bf16[4096,1024]{1,0:T(8,128)(2,1)} %fusion.4, s32[1024]{0:T(1024)S(1)} %pad_clamp_fusion.1), kind=kCustom, calls=%fused_computation.1 | custom fusion | bytes 2099200 | tf_op jit(solution)/shard_map/gather | solution.py:42
  72.8 5.7 %fusion.7 = f32[2048,1024]{1,0:T(8,128)} fusion(bf16[512,1024]{1,0:T(8,128)(2,1)S(1)} %gather_fusion.1, s32[512]{0:T(512)S(1)} %broadcast_subtract_fusion), kind=kOutput, calls=%fused_computation.21 | convolution fusion | flops 2148532224 | bytes 9439232 | tf_op jit(solution)/shard_map/dot_general | solution.py:45
  78.5 0.0 all-reduce.2.cloned.1.call-update
  78.5 0.7 copy-done.3
  79.3 0.1 copy.37
  79.4 0.6 gather_fusion.3
  80.0 0.1 reshape.291
  80.1 3.2 %fusion.5 = f32[2048]{0:T(1024)S(1)} fusion(bf16[2048,1024]{1,0:T(8,128)(2,1)} %param.9), kind=kLoop, calls=%fused_computation.16 | loop fusion | flops 6289408 | bytes 4202496 | tf_op jit(solution)/shard_map/reduce_sum | solution.py:11
  83.4 0.2 copy-done.2
  83.6 3.0 %fusion.6 = bf16[2048,1024]{1,0:T(8,128)(2,1)} fusion(bf16[2048,1024]{1,0:T(8,128)(2,1)S(1)} %copy-done.2, f32[2048]{0:T(1024)S(1)} %add_sqrt_fusion.1), kind=kLoop, calls=%fused_computation.17 | loop fusion | flops 6291456 | bytes 8396800 | tf_op jit(solution)/shard_map/convert_element_type | solution.py:11
  86.6 10.5 %gather_fusion.4 = bf16[1024,1024]{1,0:T(8,128)(2,1)} fusion(bf16[4096,1024]{1,0:T(8,128)(2,1)} %fusion.4, s32[1024]{0:T(1024)S(1)} %broadcast_clamp_fusion), kind=kCustom, calls=%fused_computation.4 | custom fusion | bytes 4198400 | tf_op jit(solution)/shard_map/gather | solution.py:57
  97.2 6.6 %all-to-all-start.1 = ((bf16[16,4,16,1024]{3,2,1,0:T(8,128)(2,1)}), bf16[16,4,16,1024]{3,2,1,0:T(8,128)(2,1)S(1)}, u32[]{:S(2)}, u32[]{:S(2)}) async-start(bf16[16,4,16,1024]{3,2,1,0:T(8,128)(2,1)} %bitcast.16), calls=%async_computation.1 | async-start | bytes 4194304 | tf_op jit(solution)/shard_map/all_to_all | solution.py:62
  103.8 40.8 %while.10 = (s32[]{:T(128)}, f32[8,512]{1,0:T(8,128)S(1)}, bf16[8,512,1024]{2,1,0:T(8,128)(2,1)}, bf16[2048,1024]{1,0:T(8,128)(2,1)}, s32[]{:T(128)}, /*index=5*/s32[]{:T(128)}) while((s32[]{:T(128)}, f32[8,512]{1,0:T(8,128)S(1)}, bf16[8,512,1024]{2,1,0:T(8,128)(2,1)}, bf16[2048,1024]{1,0:T(8,128)(2,1)}, s32[]{:T(128)}, ...), condition=%wide.region_4.5_spmd, body=%wide.region_2.4_spmd.sunk | while | flops 2148531712 | bytes 5249109 | solution.py:35
  103.8 5.0 %convolution_reduce_fusion.2 = f32[512]{0:T(512)S(1)} fusion(bf16[2048,1024]{1,0:T(8,128)(2,1)} %get-tuple-element.91, bf16[8,512,1024]{2,1,0:T(8,128)(2,1)} %get-tuple-element.90, s32[]{:T(128)S(6)} %copy.55), kind=kOutput, calls=%fused_computation.6.clone.1 | convolution fusion | flops 2148531712 | bytes 5244932 | tf_op jit(solution)/shard_map/while/body/eval_jaxpr/dot_general | solution.py:30
  108.8 0.1 dynamic_update_slice.5
  108.8 5.1 %convolution_reduce_fusion.2 = f32[512]{0:T(512)S(1)} fusion(bf16[2048,1024]{1,0:T(8,128)(2,1)} %get-tuple-element.91, bf16[8,512,1024]{2,1,0:T(8,128)(2,1)} %get-tuple-element.90, s32[]{:T(128)S(6)} %copy.55), kind=kOutput, calls=%fused_computation.6.clone.1 | convolution fusion | flops 2148531712 | bytes 5244932 | tf_op jit(solution)/shard_map/while/body/eval_jaxpr/dot_general | solution.py:30
  114.0 0.1 dynamic_update_slice.5
  114.0 5.0 %convolution_reduce_fusion.2 = f32[512]{0:T(512)S(1)} fusion(bf16[2048,1024]{1,0:T(8,128)(2,1)} %get-tuple-element.91, bf16[8,512,1024]{2,1,0:T(8,128)(2,1)} %get-tuple-element.90, s32[]{:T(128)S(6)} %copy.55), kind=kOutput, calls=%fused_computation.6.clone.1 | convolution fusion | flops 2148531712 | bytes 5244932 | tf_op jit(solution)/shard_map/while/body/eval_jaxpr/dot_general | solution.py:30
  119.0 0.1 dynamic_update_slice.5
  119.1 5.0 %convolution_reduce_fusion.2 = f32[512]{0:T(512)S(1)} fusion(bf16[2048,1024]{1,0:T(8,128)(2,1)} %get-tuple-element.91, bf16[8,512,1024]{2,1,0:T(8,128)(2,1)} %get-tuple-element.90, s32[]{:T(128)S(6)} %copy.55), kind=kOutput, calls=%fused_computation.6.clone.1 | convolution fusion | flops 2148531712 | bytes 5244932 | tf_op jit(solution)/shard_map/while/body/eval_jaxpr/dot_general | solution.py:30
  124.1 0.1 dynamic_update_slice.5
  124.2 5.0 %convolution_reduce_fusion.2 = f32[512]{0:T(512)S(1)} fusion(bf16[2048,1024]{1,0:T(8,128)(2,1)} %get-tuple-element.91, bf16[8,512,1024]{2,1,0:T(8,128)(2,1)} %get-tuple-element.90, s32[]{:T(128)S(6)} %copy.55), kind=kOutput, calls=%fused_computation.6.clone.1 | convolution fusion | flops 2148531712 | bytes 5244932 | tf_op jit(solution)/shard_map/while/body/eval_jaxpr/dot_general | solution.py:30
  129.1 0.1 dynamic_update_slice.5
  129.2 5.0 %convolution_reduce_fusion.2 = f32[512]{0:T(512)S(1)} fusion(bf16[2048,1024]{1,0:T(8,128)(2,1)} %get-tuple-element.91, bf16[8,512,1024]{2,1,0:T(8,128)(2,1)} %get-tuple-element.90, s32[]{:T(128)S(6)} %copy.55), kind=kOutput, calls=%fused_computation.6.clone.1 | convolution fusion | flops 2148531712 | bytes 5244932 | tf_op jit(solution)/shard_map/while/body/eval_jaxpr/dot_general | solution.py:30
  134.2 0.1 dynamic_update_slice.5
  134.3 5.1 %convolution_reduce_fusion.2 = f32[512]{0:T(512)S(1)} fusion(bf16[2048,1024]{1,0:T(8,128)(2,1)} %get-tuple-element.91, bf16[8,512,1024]{2,1,0:T(8,128)(2,1)} %get-tuple-element.90, s32[]{:T(128)S(6)} %copy.55), kind=kOutput, calls=%fused_computation.6.clone.1 | convolution fusion | flops 2148531712 | bytes 5244932 | tf_op jit(solution)/shard_map/while/body/eval_jaxpr/dot_general | solution.py:30
  139.4 0.1 dynamic_update_slice.5
  139.5 5.1 %convolution_reduce_fusion.2 = f32[512]{0:T(512)S(1)} fusion(bf16[2048,1024]{1,0:T(8,128)(2,1)} %get-tuple-element.91, bf16[8,512,1024]{2,1,0:T(8,128)(2,1)} %get-tuple-element.90, s32[]{:T(128)S(6)} %copy.55), kind=kOutput, calls=%fused_computation.6.clone.1 | convolution fusion | flops 2148531712 | bytes 5244932 | tf_op jit(solution)/shard_map/while/body/eval_jaxpr/dot_general | solution.py:30
  144.5 0.1 dynamic_update_slice.5
  144.6 25.4 %pmax.7 = f32[4096]{0:T(1024)} all-reduce(f32[4096]{0:T(1024)S(1)} %bitcast.49), channel_id=1, replica_groups=mesh['dp'=16,'cent'=8] {'cent'}, use_global_device_ids=true, to_apply=%region_5.6 | all-reduce | flops 4096 | bytes 32768 | tf_op jit(solution)/shard_map/pmax | solution.py:38
  170.1 0.4 compare_not_fusion
  170.5 0.1 gt.26
  170.6 0.4 and_reduce_fusion
  171.0 5.1 %select_reduce_fusion = f32[4,16,16]{2,1,0:T(8,128)S(1)} fusion(pred[16,16,16,16]{1,3,2,0:T(8,128)(4,1)S(1)} %compare_not_fusion, pred[4,16,16]{2,1,0:T(8,128)(4,1)S(1)} %copy.34, bf16[16,4,16,1024]{3,2,1,0:T(8,128)(2,1)S(1)} %all-to-all-done.1), kind=kOutput, calls=%fused_computation.18 | convolution fusion | flops 537918464 | bytes 2167808 | tf_op jit(solution)/shard_map/sgqd,tgpd->gsqtp/dot_general | solution.py:66
  176.2 0.1 reduce_max.21
  176.3 0.6 bitcast_select_fusion
  176.9 68.8 %all-reduce.2.cloned.1.call-done = f32[2048,1024]{1,0:T(8,128)} async-done(((f32[2048,1024]{1,0:T(8,128)}), f32[2048,1024]{1,0:T(8,128)}) %all-reduce.2.cloned.1.call-update) | async-done | bytes 8388624 | tf_op jit(solution)/shard_map/psum | solution.py:48
  245.7 4.0 %multiply_reduce_fusion = f32[2048]{0:T(1024)S(1)} fusion(f32[2048,1024]{1,0:T(8,128)} %all-reduce.2.cloned.1.call-done), kind=kLoop, calls=%fused_computation.19 | loop fusion | flops 4192256 | bytes 8396800 | tf_op jit(solution)/shard_map/reduce_sum | solution.py:49
  249.7 1.8 fusion.11
  251.6 1.1 copy.40
  (25 shorter events, 0.2 us)
Async XLA Ops:
  7.2 0.9 copy-start
  8.1 9.2 %copy-start.1 = (s32[4096]{0:T(1024)S(1)}, s32[4096]{0:T(1024)}, u32[]{:S(2)}) copy-start(s32[4096]{0:T(1024)} %param.10) | copy-start | bytes 49156
  9.7 87.5 %all-to-all-start = ((bf16[16,4,16]{2,1,0:T(4,128)(2,1)}), bf16[16,4,16]{2,1,0:T(4,128)(2,1)S(1)}, u32[]{:S(2)}, u32[]{:S(2)}) async-start(bf16[16,4,16]{2,1,0:T(4,128)(2,1)} %fusion.13), calls=%async_computation | async-start | bytes 32768 | tf_op jit(solution)/shard_map/all_to_all | solution.py:63
  17.3 228.4 %all-reduce.2.cloned.1.call-start = ((), (), s32[]{:S(2)}) async-start(), calls=%async_computation.2 | async-start | bytes 16777216 | tf_op jit(solution)/shard_map/psum | solution.py:48
  78.5 0.8 copy-start.3
  80.1 3.4 %copy-start.2 = (bf16[2048,1024]{1,0:T(8,128)(2,1)S(1)}, bf16[2048,1024]{1,0:T(8,128)(2,1)}, u32[]{:S(2)}) copy-start(bf16[2048,1024]{1,0:T(8,128)(2,1)} %param.9) | copy-start | bytes 12582916
  97.2 73.9 %all-to-all-start.1 = ((bf16[16,4,16,1024]{3,2,1,0:T(8,128)(2,1)}), bf16[16,4,16,1024]{3,2,1,0:T(8,128)(2,1)S(1)}, u32[]{:S(2)}, u32[]{:S(2)}) async-start(bf16[16,4,16,1024]{3,2,1,0:T(8,128)(2,1)} %bitcast.16), calls=%async_computation.1 | async-start | bytes 4194304 | tf_op jit(solution)/shard_map/all_to_all | solution.py:62
Sparse Core Ops, SparseCore 0:
  78.7 166.9 all-reduce.1
where the time goes:
time: 260 us
  waiting for transfers between devices  68.9 us (27%)
  other arithmetic  59.7 us (23%)
  matrix products  51 us (20%)
  local copies, waits for them, and re-layouts  25.8 us (10%)
  blocking collectives  25.4 us (10%)
  between operations  14.3 us (6%)
  starting transfers between devices  14.2 us (5%)
    psum x1, waiting for transfers between devices, shards(): summed = lax.psum(partial_sums, 'dp')  68.8 us
    dot_general x8, matrix products, block_best(): lax.dot_general(portion, cent_units, (((1,), (1,)), ((), ())), preferred_...  40.1 us
    scatter-add x1, other arithmetic, shards(): jnp.nonzero(in_shard, size=share_rows, fill_value=0)[0].astype(jnp.int32)  29 us
    pmax x1, blocking collectives, shards(): best_score = lax.pmax(local_best, 'cent')  25.4 us
    convert_element_type x2, other arithmetic, normalize_rows(): (wide / jnp.sqrt(jnp.sum(wide * wide, axis=1, keepdims=True) + epsilon))....  11.5 us
    gather x1, local copies, waits for them, and re-layouts, shards(): sent_rows = unit_rows[picked]  10.5 us
    reduce_sum x2, other arithmetic, normalize_rows(): jnp.sum(wide * wide, axis=1, keepdims=True) + epsilon  8.31 us
    all_to_all x1, starting transfers between devices, shards(): lax.all_to_all(sent_live, 'dp', split_axis=0, concat_axis=0, tiled=True)  7.58 us
  transfers between devices with their start and end apart: 3, of which 1 were waited for; matrix products, arithmetic and copies ran while one was open for 49% of the time, Pallas kernels for 0%

commit v1 on v0

v1 whole, which is shorter than its diff:
```python
import functools

import jax
import jax.numpy as jnp
from jax import lax
from jax.experimental import pallas as pl
from jax.experimental.pallas import tpu as pltpu
from jax.sharding import PartitionSpec as P

EPS = 1e-06
MESH = pl.DeviceIdType.MESH
F32 = jnp.float32
BF16 = jnp.bfloat16
NT = (((1,), (1,)), ((), ()))
NN = (((1,), (0,)), ((), ()))


def dot(a, b, dims):
    return lax.dot_general(a, b, dims, preferred_element_type=F32)


def body(
    og, mem, cnt, ids, emb_hbm, cent_hbm,
    best_out, new_out, slot_out,
    emb, x32, cen, g32, sb, recv, xc, cs, rc, idbuf, rid, rank, sel, ssel,
    tmax, bloc, rbest, acc, ssq, rssq,
    lsem, cl_s, cl_r, ce_s, ce_r, id_s, id_r, sq_s, sq_r, be_s, be_r,
):
    rows, feat = emb.shape
    n_dp, n_cent = 16, 8
    me = lax.axis_index("dp")
    jc = lax.axis_index("cent")
    mx, my = me // 4, lax.rem(me, 4)
    chunk = rows // 8
    share = sel.shape[0]
    cshard = cen.shape[0]
    lo_n = acc.shape[1]
    fpart = feat // n_dp

    def peer(k):
        return lax.rem(mx + k // 4, 4) * 4 + lax.rem(my + lax.rem(k, 4), 4)

    def cpeer(k):
        return lax.rem(jc + k, n_cent)

    slabs = x32.reshape(rows + 1, 8, 128)

    def load(i):
        return pltpu.make_async_copy(
            emb_hbm.at[pl.ds(i * chunk, chunk)], emb.at[pl.ds(i * chunk, chunk)], lsem.at[i]
        )

    cent_load = pltpu.make_async_copy(cent_hbm, cen, lsem.at[8])
    for i in range(8):
        load(i).start()
    cent_load.start()

    barrier = pltpu.get_barrier_semaphore()
    for k in range(1, n_dp):
        pl.semaphore_signal(barrier, inc=1, device_id={"dp": peer(k)}, device_id_type=MESH)
    for k in range(1, n_cent):
        pl.semaphore_signal(barrier, inc=1, device_id={"cent": cpeer(k)}, device_id_type=MESH)

    x32[rows * 8:, :] = jnp.full((8, 128), jnp.nan, F32)

    def widen_chunk(i, _):
        load(i).wait()

        def widen(n, _):
            r = pl.multiple_of(i * chunk + n * 16, 16)
            for c in range(8):
                v = emb[pl.ds(r, 16), c * 128:(c + 1) * 128].astype(F32)
                x32[pl.ds(r * 8 + c, 16, stride=8), :] = v
            return 0

        lax.fori_loop(0, chunk // 16, widen, 0)
        return 0

    lax.fori_loop(0, 8, widen_chunk, 0)
    pl.semaphore_wait(barrier, n_dp + n_cent - 2)

    def gather(t, p, dst):
        g = og[p * 32 + jc * 4 + t]
        live = cnt[g]
        for q in range(16):
            row = jnp.where(q < live, mem[g * 16 + q], rows)
            g32[q * 8:(q + 1) * 8, :] = slabs[row]
        for c in range(8):
            dst[:, c * 128:(c + 1) * 128] = g32[pl.ds(c, 16, stride=8), :].astype(BF16)

    def cl_copy(t, p, s):
        return pltpu.make_async_remote_copy(
            src_ref=sb.at[t, p], dst_ref=recv.at[t, s],
            send_sem=cl_s.at[t, p], recv_sem=cl_r.at[t, s],
            device_id={"dp": p}, device_id_type=MESH,
        )

    def send_round(t):
        def step(k, _):
            p = peer(k)
            gather(t, p, sb.at[t, p])
            cl_copy(t, p, me).start()
            return 0

        lax.fori_loop(1, n_dp, step, 0)
        gather(t, me, recv.at[t, me])

    send_round(0)
    send_round(1)

    idv = ids[...]
    inside = (idv // cshard) == jc
    insf = inside.astype(F32).astype(BF16)
    lane_a = lax.broadcasted_iota(jnp.int32, (128, 128), 0)
    lane_b = lax.broadcasted_iota(jnp.int32, (128, 128), 1)
    upper = (lane_a <= lane_b).astype(F32).astype(BF16)
    run = dot(insf, upper, NN)
    total = dot(insf, jnp.ones((128, 128), BF16), NN).astype(BF16)
    row_a = lax.broadcasted_iota(jnp.int32, (32, 32), 0)
    row_b = lax.broadcasted_iota(jnp.int32, (32, 32), 1)
    lower = (row_b < row_a).astype(F32).astype(BF16)
    before = dot(lower, total, NN)
    rank[0] = jnp.where(inside, before + run - 1.0, -1.0)
    local_id = idv - jc * cshard
    rank[1] = jnp.where(inside, (local_id // 256).astype(F32), 0.0)
    rank[2] = jnp.where(inside, lax.rem(local_id, 256).astype(F32), 0.0)
    xc[...] = jnp.zeros_like(xc)
    ssel[...] = jnp.zeros_like(ssel)
    want = lax.broadcasted_iota(jnp.int32, (share, 128), 0).astype(F32)
    sub16 = lax.broadcasted_iota(jnp.int32, (16, 128), 0)

    def select(n, _):
        for u in range(4):
            q = n * 4 + u
            one = (want == rank[0, pl.ds(q, 1), :]).astype(F32).astype(BF16)
            sel[:, u * 128:(u + 1) * 128] = one
            info = jnp.where(
                sub16 == 0, rank[1, pl.ds(q, 1), :],
                jnp.where(sub16 == 1, rank[2, pl.ds(q, 1), :], 0.0),
            ).astype(BF16)
            ssel[...] += dot(info, one, NT)
        r = pl.multiple_of(n * 512, 512)
        xc[...] += dot(sel[...], emb[pl.ds(r, 512), :], NN)
        return 0

    lax.fori_loop(0, 8, select, 0)
    idbuf[...] = (ssel[0:1, :] * 256.0 + ssel[1:2, :]).astype(jnp.int32)
    rid[me] = idbuf[...]

    def id_copy(p, s):
        return pltpu.make_async_remote_copy(
            src_ref=idbuf, dst_ref=rid.at[s], send_sem=id_s.at[p], recv_sem=id_r.at[s],
            device_id={"dp": p}, device_id_type=MESH,
        )

    def ce_copy(p, s):
        return pltpu.make_async_remote_copy(
            src_ref=cs.at[p], dst_ref=rc.at[s], send_sem=ce_s.at[p], recv_sem=ce_r.at[s],
            device_id={"dp": p}, device_id_type=MESH,
        )

    part = jnp.zeros((share, 128), F32)
    for c in range(8):
        v = xc[:, c * 128:(c + 1) * 128]
        part = part + v * v
    norm = jnp.sqrt(jnp.sum(part, axis=1, keepdims=True) + EPS)
    for c in range(8):
        v = (xc[:, c * 128:(c + 1) * 128] / norm).T.astype(BF16)
        cs[2 * c] = v[:fpart]
        cs[2 * c + 1] = v[fpart:]
    rc[me] = cs[me]

    def send_cent(k, _):
        p = peer(k)
        id_copy(p, me).start()
        ce_copy(p, me).start()
        return 0

    lax.fori_loop(1, n_dp, send_cent, 0)

    send_round(2)
    send_round(3)

    cent_load.wait()

    def unit_cent(n, _):
        r = pl.multiple_of(n * 128, 128)
        v = cen[pl.ds(r, 128), :].astype(F32)
        w = v / jnp.sqrt(jnp.sum(v * v, axis=1, keepdims=True) + EPS)
        cen[pl.ds(r, 128), :] = w.astype(BF16)
        return 0

    lax.fori_loop(0, cshard // 128, unit_cent, 0)

    def score(b, _):
        r = pl.multiple_of(b * 512, 512)

        def tile(n, _):
            k0 = pl.multiple_of(n * 512, 512)
            s = dot(emb[pl.ds(r, 512), :], cen[pl.ds(k0, 512), :], NT)
            m = jnp.maximum(
                jnp.maximum(s[:, 0:128], s[:, 128:256]),
                jnp.maximum(s[:, 256:384], s[:, 384:512]),
            )
            tmax[...] = jnp.where(n == 0, m, jnp.maximum(tmax[...], m))
            return 0

        lax.fori_loop(0, cshard // 512, tile, 0)
        sq = jnp.zeros((512, 128), F32)
        for c in range(8):
            v = emb[pl.ds(r, 512), c * 128:(c + 1) * 128].astype(F32)
            sq = sq + v * v
        top = jnp.max(tmax[...].T, axis=0, keepdims=True)
        nrm = jnp.sqrt(jnp.sum(sq.T, axis=0, keepdims=True) + EPS)
        bloc[pl.ds(b, 1), :] = top / nrm
        return 0

    lax.fori_loop(0, rows // 512, score, 0)

    def be_copy(p, s):
        return pltpu.make_async_remote_copy(
            src_ref=bloc, dst_ref=rbest.at[s], send_sem=be_s.at[p], recv_sem=be_r.at[s],
            device_id={"cent": p}, device_id_type=MESH,
        )

    for k in range(1, n_cent):
        be_copy(cpeer(k), jc).start()

    acc[...] = jnp.zeros_like(acc)
    want_lo = lax.broadcasted_iota(jnp.int32, (lo_n, share), 0)

    def add_rows(s):
        ident = rid[s]
        low = lax.rem(ident, lo_n)
        high = ident // lo_n
        one = (want_lo == low).astype(F32).astype(BF16)
        x = rc[s].astype(F32)
        lhs = jnp.concatenate(
            [(x * (high == h).astype(F32)).astype(BF16) for h in range(cshard // lo_n)], axis=0
        )
        acc[...] += dot(lhs, one, NT)

    def sum_step(k, _):
        s = peer(k)
        id_copy(s, s).wait_recv()
        ce_copy(s, s).wait_recv()
        add_rows(s)
        return 0

    add_rows(me)
    lax.fori_loop(1, n_dp, sum_step, 0)
    for h in range(4):
        a = acc[h * 64:(h + 1) * 64, :]
        q = jnp.sum(a * a, axis=0, keepdims=True)
        ssq[2 * h:2 * h + 1, :] = q[:, :256]
        ssq[2 * h + 1:2 * h + 2, :] = q[:, 256:]

    def sq_copy(p, s):
        return pltpu.make_async_remote_copy(
            src_ref=ssq, dst_ref=rssq.at[s], send_sem=sq_s.at[p], recv_sem=sq_r.at[s],
            device_id={"dp": p}, device_id_type=MESH,
        )

    rssq[me] = ssq[...]

    def send_sq(k, _):
        sq_copy(peer(k), me).start()
        return 0

    lax.fori_loop(1, n_dp, send_sq, 0)

    pa = lax.broadcasted_iota(jnp.int32, (256, 256), 0)
    pb = lax.broadcasted_iota(jnp.int32, (256, 256), 1)
    diag = pa == pb

    def block(t):
        def arrive(k, _):
            s = peer(k)
            cl_copy(t, s, s).wait_recv()
            return 0

        lax.fori_loop(1, n_dp, arrive, 0)
        x = recv[t].reshape(256, feat)
        gm = dot(x, x, NT)
        dg = jnp.where(diag, gm, 0.0)
        icol = 1.0 / jnp.sqrt(jnp.sum(dg, axis=1, keepdims=True) + EPS)
        irow = 1.0 / jnp.sqrt(jnp.sum(dg, axis=0, keepdims=True) + EPS)
        v = gm * icol
        ok = (v == v) & jnp.logical_not(diag)
        m = jnp.max(jnp.where(ok, v, -jnp.inf), axis=0, keepdims=True)
        slot_out[t:t + 1, :] = jnp.where(m > -jnp.inf, m * irow, -1.0)

    block(0)
    block(1)

    def got_sq(k, _):
        s = peer(k)
        sq_copy(s, s).wait_recv()
        return 0

    lax.fori_loop(1, n_dp, got_sq, 0)
    full = rssq[0]
    for s in range(1, n_dp):
        full = full + rssq[s]
    inv = 1.0 / jnp.maximum(jnp.sqrt(full), 1.0)
    for h in range(4):
        for u in range(2):
            lo = u * 256
            new_out[:, h * 512 + lo:h * 512 + lo + 256] = (
                acc[h * 64:(h + 1) * 64, lo:lo + 256] * inv[2 * h + u:2 * h + u + 1, :]
            )

    for k in range(1, n_cent):
        s = cpeer(k)
        be_copy(s, s).wait_recv()
    rbest[jc] = bloc[...]
    top = rbest[0]
    for s in range(1, n_cent):
        top = jnp.maximum(top, rbest[s])
    best_out[...] = top

    block(2)
    block(3)

    def sent(k, _):
        p = peer(k)
        for t in range(4):
            cl_copy(t, p, me).wait_send()
        id_copy(p, me).wait_send()
        ce_copy(p, me).wait_send()
        sq_copy(p, me).wait_send()
        return 0

    lax.fori_loop(1, n_dp, sent, 0)
    for k in range(1, n_cent):
        be_copy(cpeer(k), jc).wait_send()


def shards(embeddings, centroids, kmeans_id, members, counts, owner_groups):
    rows, feat = embeddings.shape
    cshard = centroids.shape[0]
    vm = pl.BlockSpec(memory_space=pltpu.VMEM)
    sm = pl.BlockSpec(memory_space=pltpu.SMEM)
    hbm = pl.BlockSpec(memory_space=pltpu.MemorySpace.HBM)
    dma = pltpu.SemaphoreType.DMA
    best, new, slot = pl.pallas_call(
        body,
        out_shape=(
            jax.ShapeDtypeStruct((8, rows // 8), F32),
            jax.ShapeDtypeStruct((feat // 16, cshard), F32),
            jax.ShapeDtypeStruct((4, 256), F32),
        ),
        in_specs=[sm, sm, sm, vm, hbm, hbm],
        out_specs=(vm, vm, vm),
        scratch_shapes=[
            pltpu.VMEM((rows, feat), BF16),
            pltpu.VMEM((rows * 8 + 8, 128), F32),
            pltpu.VMEM((cshard, feat), BF16),
            pltpu.VMEM((128, 128), F32),
            pltpu.VMEM((4, 16, 16, feat), BF16),
            pltpu.VMEM((4, 16, 16, feat), BF16),
            pltpu.VMEM((512, feat), F32),
            pltpu.VMEM((16, feat // 16, 512), BF16),
            pltpu.VMEM((16, feat // 16, 512), BF16),
            pltpu.VMEM((1, 512), jnp.int32),
            pltpu.VMEM((16, 1, 512), jnp.int32),
            pltpu.VMEM((3, 32, 128), F32),
            pltpu.VMEM((512, 512), BF16),
            pltpu.VMEM((16, 512), F32),
            pltpu.VMEM((512, 128), F32),
            pltpu.VMEM((8, rows // 8), F32),
            pltpu.VMEM((8, 8, rows // 8), F32),
            pltpu.VMEM((256, 512), F32),
            pltpu.VMEM((8, 256), F32),
            pltpu.VMEM((16, 8, 256), F32),
            dma((9,)),
            dma((4, 16)), dma((4, 16)),
            dma((16,)), dma((16,)),
            dma((16,)), dma((16,)),
            dma((16,)), dma((16,)),
            dma((8,)), dma((8,)),
        ],
        compiler_params=pltpu.CompilerParams(
            collective_id=0, has_side_effects=True, vmem_limit_bytes=58 << 20
        ),
        name="window",
    )(
        owner_groups.reshape(-1),
        members.reshape(-1),
        counts.reshape(-1),
        kmeans_id.reshape(32, 128),
        embeddings,
        centroids,
    )
    return best.reshape(rows), new, slot.reshape(1, 1, 4, 256)


def solution(mesh):
    placed = (P("dp", None), P("cent", None), P("dp"), P(None, "dp", None), P(None, "dp"), P())
    return jax.shard_map(
        shards,
        mesh=mesh,
        in_specs=placed,
        out_specs=(P("dp"), P("dp", "cent"), P("dp", "cent", None, None)),
        check_vma=False,
    )
```

time: 260 us -> 74.7 us (0.29)
  waiting for transfers between devices: 68.9 us -> 0 us
  Pallas kernels: 0 us -> 65.9 us
  other arithmetic: 59.7 us -> 0 us
  matrix products: 51 us -> 0 us
  blocking collectives: 25.4 us -> 0 us
  local copies, waits for them, and re-layouts: 25.8 us -> 7.63 us
  starting transfers between devices: 14.2 us -> 0 us
  between operations: 14.3 us -> 0.65 us
    psum x1 -> x0, waiting for transfers between devices: 68.8 us -> none  [shards(): summed = lax.psum(partial_sums, 'dp')]
    pallas_call x0 -> x1, Pallas kernels: none -> 65.9 us  [shards(): pl.pallas_call(body, out_shape=(jax.ShapeDtypeStruct((8, rows // 8), F32)...]
    dot_general x10 -> x0, matrix products: 51 us -> none  [the longest x8 40.1 us: block_best(): lax.dot_general(portion, cent_units, (((1,), (1,)), ((), ())), preferred_...]
    scatter-add x1 -> x0, other arithmetic: 29 us -> none  [shards(): jnp.nonzero(in_shard, size=share_rows, fill_value=0)[0].astype(jnp.int32)]
    pmax x1 -> x0, blocking collectives: 25.4 us -> none  [shards(): best_score = lax.pmax(local_best, 'cent')]
    gather x6 -> x0, local copies, waits for them, and re-layouts: 22.4 us -> none  [the longest x1 10.5 us: shards(): sent_rows = unit_rows[picked]]
    all_to_all x2 -> x0, starting transfers between devices: 14.2 us -> none  [the longest x1 7.58 us: shards(): lax.all_to_all(sent_live, 'dp', split_axis=0, concat_axis=0, tiled=True)]
    reduce_sum x4 -> x0, other arithmetic: 13 us -> none  [the longest x2 8.31 us: normalize_rows(): jnp.sum(wide * wide, axis=1, keepdims=True) + epsilon]
  transfers between devices with their start and end apart: 3 -> 0, of which waited for: 1 -> 0; matrix products, arithmetic and copies ran while one was open for 49% -> 0% of each run, Pallas kernels for 0% -> 0%
where the time goes in v1:
time: 74.7 us; the launch traced here: 74.1 us
  Pallas kernels  65.9 us (88%)
  local copies, waits for them, and re-layouts  7.63 us (10%)
    pallas_call x1, Pallas kernels, shards(): pl.pallas_call(body, out_shape=(jax.ShapeDtypeStruct((8, rows // 8), F32)...  65.9 us
    unnamed x5, local copies, waits for them, and re-layouts  6.19 us

profile of v1, /device:TPU:1, one launch (start us, length us, event | category | flops | bytes accessed | tf_op | source)
XLA Modules:
  0.0 74.1 jit_solution(3120633009779473483)
XLA Ops:
  0.6 0.8 %copy.9 = s32[16,8,4]{2,1,0:T(8,128)S(1)} copy(s32[16,8,4]{0,2,1:T(4,128)} %param.11) | data formatting | bytes 4096 | tf_op args[5]
  1.5 0.7 reshape.24.og
  2.2 0.9 %copy.10 = s32[512,1,16]{2,0,1:T(8,128)S(1)} copy(s32[512,1,16]{0,2,1:T(8,128)} %param.9) | data formatting | bytes 65536 | tf_op args[3]
  3.0 0.7 %reshape.25.mem = s32[8192]{0:T(1024)} reshape(s32[512,1,16]{2,0,1:T(8,128)S(1)} %copy.10) | data formatting | bytes 65536 | tf_op jit(solution)/shard_map/reshape | solution.py:389
  3.8 65.9 %window.1 = (f32[8,512]{1,0:T(8,128)}, f32[64,2048]{1,0:T(8,128)}, f32[4,256]{1,0:T(4,128)}) custom-call(s32[512]{0:T(512)} %reshape.24.og, s32[8192]{0:T(1024)} %reshape.25.mem, s32[512]{0:T(512)} %bitcast.11, s32[32,128]{1,0:T(8,128)} %bitcast.7, bf16[4096,1024]{1,0:T(8,128)(2,1)} %emb_hbm.1, bf16[2048,1024]{1,0:T(8,128)(2,1)} %cent_hbm.1), custom_call_target="tpu_custom_call" | custom-call | tf_op jit(solution)/shard_map/window/pallas_call | solution.py:346
  69.7 1.3 %copy.11 = f32[1,4,8,128]{3,1,2,0:T(4,128)} copy(f32[1,4,8,128]{3,2,1,0:T(8,128)} %bitcast.9) | data formatting | bytes 32768
  71.0 1.9 %copy.14 = f32[64,2048]{1,0:T(8,128)} copy(f32[64,2048]{1,0:T(8,128)} %get-tuple-element.13) | data formatting | bytes 1048576
  72.9 1.3 %copy.15 = f32[1,1,4,256]{3,2,1,0:T(4,128)} copy(f32[1,1,4,256]{3,2,1,0:T(4,128)} %bitcast.10) | data formatting | bytes 8192

commit v2 on v1

--- a/solution.py
+++ b/solution.py
@@ -22,7 +22,7 @@
 def body(
     og, mem, cnt, ids, emb_hbm, cent_hbm,
     best_out, new_out, slot_out,
-    emb, x32, cen, g32, sb, recv, xc, cs, rc, idbuf, rid, rank, sel, ssel,
+    emb, x32, cen, g32, sb, recv, xc, cs, rc, idbuf, rid, rank, sel, info, ssel, hot, lhs,
     tmax, bloc, rbest, acc, ssq, rssq,
     lsem, cl_s, cl_r, ce_s, ce_r, id_s, id_r, sq_s, sq_r, be_s, be_r,
 ):
@@ -73,17 +73,17 @@
                 x32[pl.ds(r * 8 + c, 16, stride=8), :] = v
             return 0
 
-        lax.fori_loop(0, chunk // 16, widen, 0)
+        lax.fori_loop(0, chunk // 16, widen, 0, unroll=4)
         return 0
 
     lax.fori_loop(0, 8, widen_chunk, 0)
     pl.semaphore_wait(barrier, n_dp + n_cent - 2)
 
     def gather(t, p, dst):
-        g = og[p * 32 + jc * 4 + t]
+        g = og[jc, t, p]
         live = cnt[g]
         for q in range(16):
-            row = jnp.where(q < live, mem[g * 16 + q], rows)
+            row = jnp.where(q < live, mem[q, g], rows)
             g32[q * 8:(q + 1) * 8, :] = slabs[row]
         for c in range(8):
             dst[:, c * 128:(c + 1) * 128] = g32[pl.ds(c, 16, stride=8), :].astype(BF16)
@@ -124,26 +124,25 @@
     local_id = idv - jc * cshard
     rank[1] = jnp.where(inside, (local_id // 256).astype(F32), 0.0)
     rank[2] = jnp.where(inside, lax.rem(local_id, 256).astype(F32), 0.0)
-    xc[...] = jnp.zeros_like(xc)
-    ssel[...] = jnp.zeros_like(ssel)
-    want = lax.broadcasted_iota(jnp.int32, (share, 128), 0).astype(F32)
+    want = lax.broadcasted_iota(jnp.int32, (256, 128), 0).astype(F32).astype(BF16)
     sub16 = lax.broadcasted_iota(jnp.int32, (16, 128), 0)
-
-    def select(n, _):
-        for u in range(4):
-            q = n * 4 + u
-            one = (want == rank[0, pl.ds(q, 1), :]).astype(F32).astype(BF16)
-            sel[:, u * 128:(u + 1) * 128] = one
-            info = jnp.where(
-                sub16 == 0, rank[1, pl.ds(q, 1), :],
-                jnp.where(sub16 == 1, rank[2, pl.ds(q, 1), :], 0.0),
-            ).astype(BF16)
-            ssel[...] += dot(info, one, NT)
-        r = pl.multiple_of(n * 512, 512)
-        xc[...] += dot(sel[...], emb[pl.ds(r, 512), :], NN)
-        return 0
-
-    lax.fori_loop(0, 8, select, 0)
+    one_b, zero_b = jnp.ones((256, 128), BF16), jnp.zeros((256, 128), BF16)
+
+    def select(q, _):
+        at = pl.ds(pl.multiple_of(q * 128, 128), 128)
+        r = rank[0, pl.ds(q, 1), :]
+        for u in range(share // 256):
+            ru = jnp.broadcast_to((r - u * 256.0).astype(BF16), (256, 128))
+            sel[u * 256:(u + 1) * 256, at] = jnp.where(want == ru, one_b, zero_b)
+        info[:, at] = jnp.where(
+            sub16 == 0, rank[1, pl.ds(q, 1), :],
+            jnp.where(sub16 == 1, rank[2, pl.ds(q, 1), :], 0.0),
+        ).astype(BF16)
+        return 0
+
+    lax.fori_loop(0, rows // 128, select, 0, unroll=4)
+    ssel[...] = dot(info[...], sel[...], NT)
+    xc[...] = dot(sel[...], emb[...], NN)
     idbuf[...] = (ssel[0:1, :] * 256.0 + ssel[1:2, :]).astype(jnp.int32)
     rid[me] = idbuf[...]
 
@@ -163,9 +162,9 @@
     for c in range(8):
         v = xc[:, c * 128:(c + 1) * 128]
         part = part + v * v
-    norm = jnp.sqrt(jnp.sum(part, axis=1, keepdims=True) + EPS)
+    scale = 1.0 / jnp.sqrt(jnp.sum(part, axis=1, keepdims=True) + EPS)
     for c in range(8):
-        v = (xc[:, c * 128:(c + 1) * 128] / norm).T.astype(BF16)
+        v = (xc[:, c * 128:(c + 1) * 128] * scale).astype(BF16).T
         cs[2 * c] = v[:fpart]
         cs[2 * c + 1] = v[fpart:]
     rc[me] = cs[me]
@@ -186,36 +185,39 @@
     def unit_cent(n, _):
         r = pl.multiple_of(n * 128, 128)
         v = cen[pl.ds(r, 128), :].astype(F32)
-        w = v / jnp.sqrt(jnp.sum(v * v, axis=1, keepdims=True) + EPS)
+        w = v * (1.0 / jnp.sqrt(jnp.sum(v * v, axis=1, keepdims=True) + EPS))
         cen[pl.ds(r, 128), :] = w.astype(BF16)
         return 0
 
     lax.fori_loop(0, cshard // 128, unit_cent, 0)
 
+    blk = tmax.shape[0]
+
     def score(b, _):
-        r = pl.multiple_of(b * 512, 512)
+        r = pl.multiple_of(b * blk, blk)
 
         def tile(n, _):
-            k0 = pl.multiple_of(n * 512, 512)
-            s = dot(emb[pl.ds(r, 512), :], cen[pl.ds(k0, 512), :], NT)
-            m = jnp.maximum(
-                jnp.maximum(s[:, 0:128], s[:, 128:256]),
-                jnp.maximum(s[:, 256:384], s[:, 384:512]),
-            )
+            k0 = pl.multiple_of(n * blk, blk)
+            s = dot(emb[pl.ds(r, blk), :], cen[pl.ds(k0, blk), :], NT)
+            m = s[:, 0:128]
+            for c in range(1, blk // 128):
+                m = jnp.maximum(m, s[:, c * 128:(c + 1) * 128])
             tmax[...] = jnp.where(n == 0, m, jnp.maximum(tmax[...], m))
             return 0
 
-        lax.fori_loop(0, cshard // 512, tile, 0)
-        sq = jnp.zeros((512, 128), F32)
+        lax.fori_loop(0, cshard // blk, tile, 0)
+        sq = jnp.zeros((blk, 128), F32)
         for c in range(8):
-            v = emb[pl.ds(r, 512), c * 128:(c + 1) * 128].astype(F32)
+            v = emb[pl.ds(r, blk), c * 128:(c + 1) * 128].astype(F32)
             sq = sq + v * v
         top = jnp.max(tmax[...].T, axis=0, keepdims=True)
         nrm = jnp.sqrt(jnp.sum(sq.T, axis=0, keepdims=True) + EPS)
-        bloc[pl.ds(b, 1), :] = top / nrm
-        return 0
-
-    lax.fori_loop(0, rows // 512, score, 0)
+        top = top / nrm
+        for c in range(blk // 128):
+            bloc[pl.ds(b * (blk // 128) + c, 1), :] = top[:, c * 128:(c + 1) * 128]
+        return 0
+
+    lax.fori_loop(0, rows // blk, score, 0)
 
     def be_copy(p, s):
         return pltpu.make_async_remote_copy(
@@ -226,34 +228,34 @@
     for k in range(1, n_cent):
         be_copy(cpeer(k), jc).start()
 
-    acc[...] = jnp.zeros_like(acc)
-    want_lo = lax.broadcasted_iota(jnp.int32, (lo_n, share), 0)
-
-    def add_rows(s):
+    n_hi = cshard // lo_n
+    want_lo = lax.broadcasted_iota(jnp.int32, (lo_n, share), 0).astype(F32).astype(BF16)
+    one_s, zero_s = jnp.ones((lo_n, share), BF16), jnp.zeros((lo_n, share), BF16)
+    zero_f = jnp.zeros((fpart, share), BF16)
+
+    def place(s, u):
         ident = rid[s]
-        low = lax.rem(ident, lo_n)
-        high = ident // lo_n
-        one = (want_lo == low).astype(F32).astype(BF16)
-        x = rc[s].astype(F32)
-        lhs = jnp.concatenate(
-            [(x * (high == h).astype(F32)).astype(BF16) for h in range(cshard // lo_n)], axis=0
-        )
-        acc[...] += dot(lhs, one, NT)
-
-    def sum_step(k, _):
+        low = (ident & (lo_n - 1)).astype(F32).astype(BF16)
+        high = (ident // lo_n).astype(F32).astype(BF16)
+        at = slice(u * share, (u + 1) * share)
+        hot[:, at] = jnp.where(want_lo == jnp.broadcast_to(low, (lo_n, share)), one_s, zero_s)
+        x = rc[s]
+        hb = jnp.broadcast_to(high, (fpart, share))
+        for h in range(n_hi):
+            lhs[h * fpart:(h + 1) * fpart, at] = jnp.where(hb == float(h), x, zero_f)
+
+    for k in range(n_dp):
         s = peer(k)
-        id_copy(s, s).wait_recv()
-        ce_copy(s, s).wait_recv()
-        add_rows(s)
-        return 0
-
-    add_rows(me)
-    lax.fori_loop(1, n_dp, sum_step, 0)
-    for h in range(4):
-        a = acc[h * 64:(h + 1) * 64, :]
-        q = jnp.sum(a * a, axis=0, keepdims=True)
-        ssq[2 * h:2 * h + 1, :] = q[:, :256]
-        ssq[2 * h + 1:2 * h + 2, :] = q[:, 256:]
+        if k > 0:
+            id_copy(s, s).wait_recv()
+            ce_copy(s, s).wait_recv()
+        place(s, k % 4)
+        if k % 4 == 3:
+            add = dot(lhs[...], hot[...], NT)
+            acc[...] = add if k == 3 else acc[...] + add
+    for h in range(n_hi):
+        a = acc[h * fpart:(h + 1) * fpart, :]
+        ssq[h:h + 1, :] = jnp.sum(a * a, axis=0, keepdims=True)
 
     def sq_copy(p, s):
         return pltpu.make_async_remote_copy(
@@ -303,12 +305,10 @@
     for s in range(1, n_dp):
         full = full + rssq[s]
     inv = 1.0 / jnp.maximum(jnp.sqrt(full), 1.0)
-    for h in range(4):
-        for u in range(2):
-            lo = u * 256
-            new_out[:, h * 512 + lo:h * 512 + lo + 256] = (
-                acc[h * 64:(h + 1) * 64, lo:lo + 256] * inv[2 * h + u:2 * h + u + 1, :]
-            )
+    for h in range(n_hi):
+        new_out[:, h * lo_n:(h + 1) * lo_n] = (
+            acc[h * fpart:(h + 1) * fpart, :] * inv[h:h + 1, :]
+        )
 
     for k in range(1, n_cent):
         s = cpeer(k)
@@ -334,6 +334,15 @@
     lax.fori_loop(1, n_dp, sent, 0)
     for k in range(1, n_cent):
         be_copy(cpeer(k), jc).wait_send()
+
+
+def hand_over(best, new, slot, best_out, new_out, slot_out, sems):
+    pairs = ((new, new_out), (best, best_out), (slot, slot_out))
+    copies = [pltpu.make_async_copy(a, b, sems.at[i]) for i, (a, b) in enumerate(pairs)]
+    for c in copies:
+        c.start()
+    for c in copies:
+        c.wait()
 
 
 def shards(embeddings, centroids, kmeans_id, members, counts, owner_groups):
@@ -346,7 +355,7 @@
     best, new, slot = pl.pallas_call(
         body,
         out_shape=(
-            jax.ShapeDtypeStruct((8, rows // 8), F32),
+            jax.ShapeDtypeStruct((rows // 128, 128), F32),
             jax.ShapeDtypeStruct((feat // 16, cshard), F32),
             jax.ShapeDtypeStruct((4, 256), F32),
         ),
@@ -365,12 +374,15 @@
             pltpu.VMEM((1, 512), jnp.int32),
             pltpu.VMEM((16, 1, 512), jnp.int32),
             pltpu.VMEM((3, 32, 128), F32),
-            pltpu.VMEM((512, 512), BF16),
+            pltpu.VMEM((512, rows), BF16),
+            pltpu.VMEM((16, rows), BF16),
             pltpu.VMEM((16, 512), F32),
-            pltpu.VMEM((512, 128), F32),
-            pltpu.VMEM((8, rows // 8), F32),
-            pltpu.VMEM((8, 8, rows // 8), F32),
-            pltpu.VMEM((256, 512), F32),
+            pltpu.VMEM((256, 2048), BF16),
+            pltpu.VMEM((512, 2048), BF16),
+            pltpu.VMEM((1024, 128), F32),
+            pltpu.VMEM((rows // 128, 128), F32),
+            pltpu.VMEM((8, rows // 128, 128), F32),
+            pltpu.VMEM((512, 256), F32),
             pltpu.VMEM((8, 256), F32),
             pltpu.VMEM((16, 8, 256), F32),
             dma((9,)),
@@ -385,13 +397,21 @@
         ),
         name="window",
     )(
-        owner_groups.reshape(-1),
-        members.reshape(-1),
+        owner_groups.transpose(1, 2, 0),
+        members[:, 0, :].T,
         counts.reshape(-1),
         kmeans_id.reshape(32, 128),
         embeddings,
         centroids,
     )
+    best, new, slot = pl.pallas_call(
+        hand_over,
+        out_shape=tuple(jax.ShapeDtypeStruct(v.shape, v.dtype) for v in (best, new, slot)),
+        in_specs=[hbm, hbm, hbm],
+        out_specs=(hbm, hbm, hbm),
+        scratch_shapes=[dma((3,))],
+        name="hand_over",
+    )(best, new, slot)
     return best.reshape(rows), new, slot.reshape(1, 1, 4, 256)
 
 

time: 74.7 us -> 78.4 us (1.050)
  Pallas kernels: 65.9 us -> 77.5 us
  local copies, waits for them, and re-layouts: 7.63 us -> 0 us
    pallas_call x1 -> x2, Pallas kernels: 65.9 us -> 77.5 us  [the longest x1 59.9 us: shards(): pl.pallas_call(body, out_shape=(jax.ShapeDtypeStruct((rows // 128, 128),...]
    unnamed x5 -> x0, local copies, waits for them, and re-layouts: 6.19 us -> none
    reshape x2 -> x0, local copies, waits for them, and re-layouts: 1.43 us -> none  [the longest x1 0.75 us: shards(): members.reshape(-1)]
where the time goes in v2:
time: 78.4 us; the launch traced here: 78.1 us
  Pallas kernels  77.5 us (99%)
    pallas_call x1, Pallas kernels, shards(): pl.pallas_call(body, out_shape=(jax.ShapeDtypeStruct((rows // 128, 128),...  59.9 us
    pallas_call x1, Pallas kernels, shards(): pl.pallas_call(hand_over, out_shape=tuple((jax.ShapeDtypeStruct(v.shape,...  17.6 us

profile of v2, /device:TPU:1, one launch (start us, length us, event | category | flops | bytes accessed | tf_op | source)
XLA Modules:
  0.0 78.1 jit_solution(1675132481839719031)
XLA Ops:
  0.6 59.9 %window.1 = (f32[32,128]{1,0:T(8,128)}, f32[64,2048]{1,0:T(8,128)}, f32[4,256]{1,0:T(4,128)}) custom-call(s32[8,4,16]{2,1,0:T(4,128)} %bitcast.9, s32[16,512]{1,0:T(8,128)} %bitcast.8, s32[512]{0:T(512)} %bitcast.11, s32[32,128]{1,0:T(8,128)} %bitcast.10, bf16[4096,1024]{1,0:T(8,128)(2,1)} %emb_hbm.1, bf16[2048,1024]{1,0:T(8,128)(2,1)} %cent_hbm.1), custom_call_target="tpu_custom_call" | custom-call | tf_op jit(solution)/shard_map/window/pallas_call | solution.py:355
  60.5 17.6 %hand_over.1 = (f32[32,128]{1,0:T(8,128)}, f32[64,2048]{1,0:T(8,128)}, f32[4,256]{1,0:T(4,128)}) custom-call(f32[32,128]{1,0:T(8,128)} %get-tuple-element.9.best, f32[64,2048]{1,0:T(8,128)} %get-tuple-element.10.new, f32[4,256]{1,0:T(4,128)} %get-tuple-element.11.slot), custom_call_target="tpu_custom_call" | custom-call | tf_op jit(solution)/shard_map/hand_over/pallas_call | solution.py:407

commit v3 on v2

--- a/solution.py
+++ b/solution.py
@@ -336,13 +336,10 @@
         be_copy(cpeer(k), jc).wait_send()
 
 
-def hand_over(best, new, slot, best_out, new_out, slot_out, sems):
-    pairs = ((new, new_out), (best, best_out), (slot, slot_out))
-    copies = [pltpu.make_async_copy(a, b, sems.at[i]) for i, (a, b) in enumerate(pairs)]
-    for c in copies:
-        c.start()
-    for c in copies:
-        c.wait()
+def hand_over(best, new, slot, best_out, new_out, slot_out):
+    best_out[...] = best[...]
+    new_out[...] = new[...]
+    slot_out[...] = slot[...]
 
 
 def shards(embeddings, centroids, kmeans_id, members, counts, owner_groups):
@@ -407,9 +404,9 @@
     best, new, slot = pl.pallas_call(
         hand_over,
         out_shape=tuple(jax.ShapeDtypeStruct(v.shape, v.dtype) for v in (best, new, slot)),
-        in_specs=[hbm, hbm, hbm],
-        out_specs=(hbm, hbm, hbm),
-        scratch_shapes=[dma((3,))],
+        in_specs=[vm, vm, vm],
+        out_specs=(vm, vm, vm),
+        compiler_params=pltpu.CompilerParams(vmem_limit_bytes=4 << 20),
         name="hand_over",
     )(best, new, slot)
     return best.reshape(rows), new, slot.reshape(1, 1, 4, 256)

time: 78.4 us -> 64.1 us (0.82)
  Pallas kernels: 77.5 us -> 60.7 us
  local copies, waits for them, and re-layouts: 0 us -> 2.42 us
    pallas_call x1, Pallas kernels: 17.6 us -> 0.83 us  [shards(): pl.pallas_call(hand_over, out_shape=tuple((jax.ShapeDtypeStruct(v.shape,...]
    unnamed x0 -> x6, local copies, waits for them, and re-layouts: none -> 2.42 us
where the time goes in v3:
time: 64.1 us; the launch traced here: 63.8 us
  Pallas kernels  60.7 us (95%)
  local copies, waits for them, and re-layouts  2.42 us (4%)
  between operations  0.65 us (1%)
    pallas_call x1, Pallas kernels, shards(): pl.pallas_call(body, out_shape=(jax.ShapeDtypeStruct((rows // 128, 128),...  59.9 us
    unnamed x6, local copies, waits for them, and re-layouts  2.42 us

profile of v3, /device:TPU:1, one launch (start us, length us, event | category | flops | bytes accessed | tf_op | source)
XLA Modules:
  0.0 63.8 jit_solution(14637674225361599605)
XLA Ops:
  0.6 59.9 %window.1 = (f32[32,128]{1,0:T(8,128)}, f32[64,2048]{1,0:T(8,128)}, f32[4,256]{1,0:T(4,128)}) custom-call(s32[8,4,16]{2,1,0:T(4,128)} %bitcast.9, s32[16,512]{1,0:T(8,128)} %bitcast.8, s32[512]{0:T(512)} %bitcast.11, s32[32,128]{1,0:T(8,128)} %bitcast.10, bf16[4096,1024]{1,0:T(8,128)(2,1)} %emb_hbm.1, bf16[2048,1024]{1,0:T(8,128)(2,1)} %cent_hbm.1), custom_call_target="tpu_custom_call" | custom-call | tf_op jit(solution)/shard_map/window/pallas_call | solution.py:352
  60.5 0.0 copy-start
  60.5 1.0 %copy-done = f32[64,2048]{1,0:T(8,128)S(1)} copy-done((f32[64,2048]{1,0:T(8,128)S(1)}, f32[64,2048]{1,0:T(8,128)}, u32[]{:S(2)}) %copy-start) | copy-done | bytes 524312
  61.6 0.0 copy-start.1
  61.6 0.7 %copy-done.1 = f32[32,128]{1,0:T(8,128)S(1)} copy-done((f32[32,128]{1,0:T(8,128)S(1)}, f32[32,128]{1,0:T(8,128)}, u32[]{:S(2)}) %copy-start.1) | copy-done | bytes 16408
  62.3 0.0 copy-start.2
  62.3 0.7 %copy-done.2 = f32[4,256]{1,0:T(4,128)S(1)} copy-done((f32[4,256]{1,0:T(4,128)S(1)}, f32[4,256]{1,0:T(4,128)}, u32[]{:S(2)}) %copy-start.2) | copy-done | bytes 4120
  62.9 0.8 %hand_over.1 = (f32[32,128]{1,0:T(8,128)}, f32[64,2048]{1,0:T(8,128)}, f32[4,256]{1,0:T(4,128)}) custom-call(f32[32,128]{1,0:T(8,128)S(1)} %copy-done.1, f32[64,2048]{1,0:T(8,128)S(1)} %copy-done, f32[4,256]{1,0:T(4,128)S(1)} %copy-done.2), custom_call_target="tpu_custom_call" | custom-call | tf_op jit(solution)/shard_map/hand_over/pallas_call | solution.py:404
Async XLA Ops:
  60.5 1.0 %copy-start = (f32[64,2048]{1,0:T(8,128)S(1)}, f32[64,2048]{1,0:T(8,128)}, u32[]{:S(2)}) copy-start(f32[64,2048]{1,0:T(8,128)} %get-tuple-element.10.new) | copy-start | bytes 1572868
  61.6 0.7 %copy-start.1 = (f32[32,128]{1,0:T(8,128)S(1)}, f32[32,128]{1,0:T(8,128)}, u32[]{:S(2)}) copy-start(f32[32,128]{1,0:T(8,128)} %get-tuple-element.9.best) | copy-start | bytes 49156
  62.3 0.7 %copy-start.2 = (f32[4,256]{1,0:T(4,128)S(1)}, f32[4,256]{1,0:T(4,128)}, u32[]{:S(2)}) copy-start(f32[4,256]{1,0:T(4,128)} %get-tuple-element.11.slot) | copy-start | bytes 12292

commit v4 on v3

--- a/solution.py
+++ b/solution.py
@@ -20,9 +20,9 @@
 
 
 def body(
-    og, mem, cnt, ids, emb_hbm, cent_hbm,
+    og_hbm, mem_hbm, cnt_hbm, ids_hbm, emb_hbm, cent_hbm,
     best_out, new_out, slot_out,
-    emb, x32, cen, g32, sb, recv, xc, cs, rc, idbuf, rid, rank, sel, info, ssel, hot, lhs,
+    og, mem, cnt, ids, pick, emb, x32, sqp, cen, g32, sb, recv, xc, cs, rc, idbuf, lbuf, rid, rank, sel, info, ssel, hot, lhs,
     tmax, bloc, rbest, acc, ssq, rssq,
     lsem, cl_s, cl_r, ce_s, ce_r, id_s, id_r, sq_s, sq_r, be_s, be_r,
 ):
@@ -32,7 +32,7 @@
     jc = lax.axis_index("cent")
     mx, my = me // 4, lax.rem(me, 4)
     chunk = rows // 8
-    share = sel.shape[0]
+    share = pick.shape[1]
     cshard = cen.shape[0]
     lo_n = acc.shape[1]
     fpart = feat // n_dp
@@ -51,9 +51,14 @@
         )
 
     cent_load = pltpu.make_async_copy(cent_hbm, cen, lsem.at[8])
+    tables = [
+        pltpu.make_async_copy(a, b, lsem.at[9 + i])
+        for i, (a, b) in enumerate(((og_hbm, og), (mem_hbm, mem), (cnt_hbm, cnt), (ids_hbm, ids)))
+    ]
+    for c in tables:
+        c.start()
     for i in range(8):
         load(i).start()
-    cent_load.start()
 
     barrier = pltpu.get_barrier_semaphore()
     for k in range(1, n_dp):
@@ -68,15 +73,21 @@
 
         def widen(n, _):
             r = pl.multiple_of(i * chunk + n * 16, 16)
+            square = jnp.zeros((16, 128), F32)
             for c in range(8):
                 v = emb[pl.ds(r, 16), c * 128:(c + 1) * 128].astype(F32)
                 x32[pl.ds(r * 8 + c, 16, stride=8), :] = v
+                square = square + v * v
+            sqp[pl.ds(r, 16), :] = square
             return 0
 
         lax.fori_loop(0, chunk // 16, widen, 0, unroll=4)
         return 0
 
     lax.fori_loop(0, 8, widen_chunk, 0)
+    cent_load.start()
+    for c in tables:
+        c.wait()
     pl.semaphore_wait(barrier, n_dp + n_cent - 2)
 
     def gather(t, p, dst):
@@ -99,14 +110,17 @@
         def step(k, _):
             p = peer(k)
             gather(t, p, sb.at[t, p])
-            cl_copy(t, p, me).start()
+
+            @pl.when(k > 0)
+            def _():
+                cl_copy(t, p, me).start()
+
             return 0
 
-        lax.fori_loop(1, n_dp, step, 0)
-        gather(t, me, recv.at[t, me])
+        lax.fori_loop(0, n_dp, step, 0)
+        recv[t, me] = sb[t, me]
 
     send_round(0)
-    send_round(1)
 
     idv = ids[...]
     inside = (idv // cshard) == jc
@@ -126,24 +140,32 @@
     rank[2] = jnp.where(inside, lax.rem(local_id, 256).astype(F32), 0.0)
     want = lax.broadcasted_iota(jnp.int32, (256, 128), 0).astype(F32).astype(BF16)
     sub16 = lax.broadcasted_iota(jnp.int32, (16, 128), 0)
+    lane16 = lax.broadcasted_iota(jnp.int32, (16, 128), 1)
     one_b, zero_b = jnp.ones((256, 128), BF16), jnp.zeros((256, 128), BF16)
-
-    def select(q, _):
-        at = pl.ds(pl.multiple_of(q * 128, 128), 128)
-        r = rank[0, pl.ds(q, 1), :]
-        for u in range(share // 256):
-            ru = jnp.broadcast_to((r - u * 256.0).astype(BF16), (256, 128))
-            sel[u * 256:(u + 1) * 256, at] = jnp.where(want == ru, one_b, zero_b)
-        info[:, at] = jnp.where(
-            sub16 == 0, rank[1, pl.ds(q, 1), :],
-            jnp.where(sub16 == 1, rank[2, pl.ds(q, 1), :], 0.0),
-        ).astype(BF16)
-        return 0
-
-    lax.fori_loop(0, rows // 128, select, 0, unroll=4)
-    ssel[...] = dot(info[...], sel[...], NT)
-    xc[...] = dot(sel[...], emb[...], NN)
-    idbuf[...] = (ssel[0:1, :] * 256.0 + ssel[1:2, :]).astype(jnp.int32)
+    ssel[...] = jnp.zeros_like(ssel)
+
+    def select(n, _):
+        for v in range(4):
+            q = n * 4 + v
+            at = slice(v * 128, (v + 1) * 128)
+            r = rank[0, pl.ds(q, 1), :]
+            for u in range(share // 256):
+                ru = jnp.broadcast_to((r - u * 256.0).astype(BF16), (256, 128))
+                sel[u * 256:(u + 1) * 256, at] = jnp.where(want == ru, one_b, zero_b)
+            place_hi = jnp.zeros((16, 128), jnp.int32) + (n * 2 + v // 2)
+            place_lo = lane16 + (v % 2) * 128
+            value = jnp.where(sub16 == 0, place_hi, place_lo).astype(F32)
+            value = jnp.where(sub16 == 2, rank[1, pl.ds(q, 1), :], value)
+            value = jnp.where(sub16 == 3, rank[2, pl.ds(q, 1), :], value)
+            info[:, at] = value.astype(BF16)
+        ssel[...] += dot(info[...], sel[...], NT)
+        return 0
+
+    lax.fori_loop(0, rows // 512, select, 0)
+    lbuf[...] = (ssel[0:1, :] * 256.0 + ssel[1:2, :]).astype(jnp.int32)
+    to_smem = pltpu.make_async_copy(lbuf, pick, lsem.at[13])
+    to_smem.start()
+    idbuf[...] = (ssel[2:3, :] * 256.0 + ssel[3:4, :]).astype(jnp.int32)
     rid[me] = idbuf[...]
 
     def id_copy(p, s):
@@ -158,13 +180,22 @@
             device_id={"dp": p}, device_id_type=MESH,
         )
 
+    to_smem.wait()
+
+    def take(n, _):
+        for u in range(16):
+            p = n * 16 + u
+            xc[pl.ds(pl.multiple_of(p * 8, 8), 8), :] = slabs[jnp.clip(pick[0, p], 0, rows - 1)]
+        return 0
+
+    lax.fori_loop(0, share // 16, take, 0)
     part = jnp.zeros((share, 128), F32)
     for c in range(8):
-        v = xc[:, c * 128:(c + 1) * 128]
+        v = xc[pl.ds(c, share, stride=8), :]
         part = part + v * v
     scale = 1.0 / jnp.sqrt(jnp.sum(part, axis=1, keepdims=True) + EPS)
     for c in range(8):
-        v = (xc[:, c * 128:(c + 1) * 128] * scale).astype(BF16).T
+        v = (xc[pl.ds(c, share, stride=8), :] * scale).astype(BF16).T
         cs[2 * c] = v[:fpart]
         cs[2 * c + 1] = v[fpart:]
     rc[me] = cs[me]
@@ -177,8 +208,11 @@
 
     lax.fori_loop(1, n_dp, send_cent, 0)
 
-    send_round(2)
-    send_round(3)
+    def later_round(t, _):
+        send_round(t)
+        return 0
+
+    lax.fori_loop(1, 4, later_round, 0)
 
     cent_load.wait()
 
@@ -191,42 +225,11 @@
 
     lax.fori_loop(0, cshard // 128, unit_cent, 0)
 
-    blk = tmax.shape[0]
-
-    def score(b, _):
-        r = pl.multiple_of(b * blk, blk)
-
-        def tile(n, _):
-            k0 = pl.multiple_of(n * blk, blk)
-            s = dot(emb[pl.ds(r, blk), :], cen[pl.ds(k0, blk), :], NT)
-            m = s[:, 0:128]
-            for c in range(1, blk // 128):
-                m = jnp.maximum(m, s[:, c * 128:(c + 1) * 128])
-            tmax[...] = jnp.where(n == 0, m, jnp.maximum(tmax[...], m))
-            return 0
-
-        lax.fori_loop(0, cshard // blk, tile, 0)
-        sq = jnp.zeros((blk, 128), F32)
-        for c in range(8):
-            v = emb[pl.ds(r, blk), c * 128:(c + 1) * 128].astype(F32)
-            sq = sq + v * v
-        top = jnp.max(tmax[...].T, axis=0, keepdims=True)
-        nrm = jnp.sqrt(jnp.sum(sq.T, axis=0, keepdims=True) + EPS)
-        top = top / nrm
-        for c in range(blk // 128):
-            bloc[pl.ds(b * (blk // 128) + c, 1), :] = top[:, c * 128:(c + 1) * 128]
-        return 0
-
-    lax.fori_loop(0, rows // blk, score, 0)
-
-    def be_copy(p, s):
+    def sq_copy(p, s):
         return pltpu.make_async_remote_copy(
-            src_ref=bloc, dst_ref=rbest.at[s], send_sem=be_s.at[p], recv_sem=be_r.at[s],
-            device_id={"cent": p}, device_id_type=MESH,
-        )
-
-    for k in range(1, n_cent):
-        be_copy(cpeer(k), jc).start()
+            src_ref=ssq, dst_ref=rssq.at[s], send_sem=sq_s.at[p], recv_sem=sq_r.at[s],
+            device_id={"dp": p}, device_id_type=MESH,
+        )
 
     n_hi = cshard // lo_n
     want_lo = lax.broadcasted_iota(jnp.int32, (lo_n, share), 0).astype(F32).astype(BF16)
@@ -244,38 +247,72 @@
         for h in range(n_hi):
             lhs[h * fpart:(h + 1) * fpart, at] = jnp.where(hb == float(h), x, zero_f)
 
-    for k in range(n_dp):
+    def arrived(k, _):
         s = peer(k)
-        if k > 0:
-            id_copy(s, s).wait_recv()
-            ce_copy(s, s).wait_recv()
-        place(s, k % 4)
-        if k % 4 == 3:
-            add = dot(lhs[...], hot[...], NT)
-            acc[...] = add if k == 3 else acc[...] + add
-    for h in range(n_hi):
-        a = acc[h * fpart:(h + 1) * fpart, :]
-        ssq[h:h + 1, :] = jnp.sum(a * a, axis=0, keepdims=True)
-
-    def sq_copy(p, s):
+        id_copy(s, s).wait_recv()
+        ce_copy(s, s).wait_recv()
+        return 0
+
+    def add_group(g, _):
+        for u in range(4):
+            place(peer(g * 4 + u), u)
+        acc[...] += dot(lhs[...], hot[...], NT)
+        return 0
+
+    def sum_rows():
+        lax.fori_loop(1, n_dp, arrived, 0)
+        acc[...] = jnp.zeros_like(acc)
+        lax.fori_loop(0, 4, add_group, 0)
+        for h in range(n_hi):
+            a = acc[h * fpart:(h + 1) * fpart, :]
+            ssq[h:h + 1, :] = jnp.sum(a * a, axis=0, keepdims=True)
+        rssq[me] = ssq[...]
+
+        def send_sq(k, _):
+            sq_copy(peer(k), me).start()
+            return 0
+
+        lax.fori_loop(1, n_dp, send_sq, 0)
+
+    blk = tmax.shape[0]
+
+    def score(b, _):
+        pl.when(b == rows // blk - 1)(sum_rows)
+        r = pl.multiple_of(b * blk, blk)
+
+        def tile(n, _):
+            k0 = pl.multiple_of(n * blk, blk)
+            s = dot(emb[pl.ds(r, blk), :], cen[pl.ds(k0, blk), :], NT)
+            m = s[:, 0:128]
+            for c in range(1, blk // 128):
+                m = jnp.maximum(m, s[:, c * 128:(c + 1) * 128])
+            tmax[...] = jnp.where(n == 0, m, jnp.maximum(tmax[...], m))
+            return 0
+
+        lax.fori_loop(0, cshard // blk, tile, 0)
+        top = jnp.max(tmax[...].T, axis=0, keepdims=True)
+        nrm = jnp.sqrt(jnp.sum(sqp[pl.ds(r, blk), :].T, axis=0, keepdims=True) + EPS)
+        top = top / nrm
+        for c in range(blk // 128):
+            bloc[pl.ds(b * (blk // 128) + c, 1), :] = top[:, c * 128:(c + 1) * 128]
+        return 0
+
+    lax.fori_loop(0, rows // blk, score, 0)
+
+    def be_copy(p, s):
         return pltpu.make_async_remote_copy(
-            src_ref=ssq, dst_ref=rssq.at[s], send_sem=sq_s.at[p], recv_sem=sq_r.at[s],
-            device_id={"dp": p}, device_id_type=MESH,
-        )
-
-    rssq[me] = ssq[...]
-
-    def send_sq(k, _):
-        sq_copy(peer(k), me).start()
-        return 0
-
-    lax.fori_loop(1, n_dp, send_sq, 0)
+            src_ref=bloc, dst_ref=rbest.at[s], send_sem=be_s.at[p], recv_sem=be_r.at[s],
+            device_id={"cent": p}, device_id_type=MESH,
+        )
+
+    for k in range(1, n_cent):
+        be_copy(cpeer(k), jc).start()
 
     pa = lax.broadcasted_iota(jnp.int32, (256, 256), 0)
     pb = lax.broadcasted_iota(jnp.int32, (256, 256), 1)
     diag = pa == pb
 
-    def block(t):
+    def block(t, _):
         def arrive(k, _):
             s = peer(k)
             cl_copy(t, s, s).wait_recv()
@@ -290,10 +327,8 @@
         v = gm * icol
         ok = (v == v) & jnp.logical_not(diag)
         m = jnp.max(jnp.where(ok, v, -jnp.inf), axis=0, keepdims=True)
-        slot_out[t:t + 1, :] = jnp.where(m > -jnp.inf, m * irow, -1.0)
-
-    block(0)
-    block(1)
+        slot_out[pl.ds(t, 1), :] = jnp.where(m > -jnp.inf, m * irow, -1.0)
+        return 0
 
     def got_sq(k, _):
         s = peer(k)
@@ -319,8 +354,7 @@
         top = jnp.maximum(top, rbest[s])
     best_out[...] = top
 
-    block(2)
-    block(3)
+    lax.fori_loop(0, 4, block, 0)
 
     def sent(k, _):
         p = peer(k)
@@ -346,9 +380,12 @@
     rows, feat = embeddings.shape
     cshard = centroids.shape[0]
     vm = pl.BlockSpec(memory_space=pltpu.VMEM)
-    sm = pl.BlockSpec(memory_space=pltpu.SMEM)
     hbm = pl.BlockSpec(memory_space=pltpu.MemorySpace.HBM)
     dma = pltpu.SemaphoreType.DMA
+    tables = (
+        owner_groups.transpose(1, 2, 0), members[:, 0, :].T,
+        counts.reshape(-1), kmeans_id.reshape(32, 128),
+    )
     best, new, slot = pl.pallas_call(
         body,
         out_shape=(
@@ -356,23 +393,30 @@
             jax.ShapeDtypeStruct((feat // 16, cshard), F32),
             jax.ShapeDtypeStruct((4, 256), F32),
         ),
-        in_specs=[sm, sm, sm, vm, hbm, hbm],
+        in_specs=[hbm] * 6,
         out_specs=(vm, vm, vm),
         scratch_shapes=[
+            pltpu.SMEM((8, 4, 16), jnp.int32),
+            pltpu.SMEM((16, 512), jnp.int32),
+            pltpu.SMEM((512,), jnp.int32),
+            pltpu.VMEM((rows // 128, 128), jnp.int32),
+            pltpu.SMEM((1, 512), jnp.int32),
             pltpu.VMEM((rows, feat), BF16),
             pltpu.VMEM((rows * 8 + 8, 128), F32),
+            pltpu.VMEM((rows, 128), F32),
             pltpu.VMEM((cshard, feat), BF16),
             pltpu.VMEM((128, 128), F32),
             pltpu.VMEM((4, 16, 16, feat), BF16),
             pltpu.VMEM((4, 16, 16, feat), BF16),
-            pltpu.VMEM((512, feat), F32),
+            pltpu.VMEM((512 * 8, 128), F32),
             pltpu.VMEM((16, feat // 16, 512), BF16),
             pltpu.VMEM((16, feat // 16, 512), BF16),
             pltpu.VMEM((1, 512), jnp.int32),
+            pltpu.VMEM((1, 512), jnp.int32),
             pltpu.VMEM((16, 1, 512), jnp.int32),
             pltpu.VMEM((3, 32, 128), F32),
-            pltpu.VMEM((512, rows), BF16),
-            pltpu.VMEM((16, rows), BF16),
+            pltpu.VMEM((512, 512), BF16),
+            pltpu.VMEM((16, 512), BF16),
             pltpu.VMEM((16, 512), F32),
             pltpu.VMEM((256, 2048), BF16),
             pltpu.VMEM((512, 2048), BF16),
@@ -382,7 +426,7 @@
             pltpu.VMEM((512, 256), F32),
             pltpu.VMEM((8, 256), F32),
             pltpu.VMEM((16, 8, 256), F32),
-            dma((9,)),
+            dma((14,)),
             dma((4, 16)), dma((4, 16)),
             dma((16,)), dma((16,)),
             dma((16,)), dma((16,)),
@@ -390,14 +434,11 @@
             dma((8,)), dma((8,)),
         ],
         compiler_params=pltpu.CompilerParams(
-            collective_id=0, has_side_effects=True, vmem_limit_bytes=58 << 20
+            collective_id=0, has_side_effects=True, vmem_limit_bytes=50 << 20
         ),
         name="window",
     )(
-        owner_groups.transpose(1, 2, 0),
-        members[:, 0, :].T,
-        counts.reshape(-1),
-        kmeans_id.reshape(32, 128),
+        *(pltpu.with_memory_space_constraint(v, pltpu.MemorySpace.HBM) for v in tables),
         embeddings,
         centroids,
     )

time: 64.1 us -> 56.4 us (0.88)
  Pallas kernels: 60.7 us -> 55.7 us
  local copies, waits for them, and re-layouts: 2.42 us -> 0 us
    pallas_call x1, Pallas kernels: 59.9 us -> 54.8 us  [shards(): pl.pallas_call(body, out_shape=(jax.ShapeDtypeStruct((rows // 128, 128),...]
    unnamed x6 -> x0, local copies, waits for them, and re-layouts: 2.42 us -> none
where the time goes in v4:
time: 56.4 us; the launch traced here: 56.3 us
  Pallas kernels  55.7 us (99%)
  between operations  0.64 us (1%)
    pallas_call x1, Pallas kernels, shards(): pl.pallas_call(body, out_shape=(jax.ShapeDtypeStruct((rows // 128, 128),...  54.8 us

profile of v4, /device:TPU:1, one launch (start us, length us, event | category | flops | bytes accessed | tf_op | source)
XLA Modules:
  0.0 56.3 jit_solution(14314616094665281732)
XLA Ops:
  0.6 54.8 %window.1 = (f32[32,128]{1,0:T(8,128)S(1)}, f32[64,2048]{1,0:T(8,128)S(1)}, f32[4,256]{1,0:T(4,128)S(1)}) custom-call(s32[8,4,16]{2,1,0:T(4,128)} %bitcast.9, s32[16,512]{1,0:T(8,128)} %bitcast.8, s32[512]{0:T(512)} %bitcast.11, s32[32,128]{1,0:T(8,128)} %bitcast.10, bf16[4096,1024]{1,0:T(8,128)(2,1)} %emb_hbm.1, bf16[2048,1024]{1,0:T(8,128)(2,1)} %cent_hbm.1), custom_call_target="tpu_custom_call" | custom-call | tf_op jit(solution)/shard_map/window/pallas_call | solution.py:389
  55.5 0.8 %hand_over.1 = (f32[32,128]{1,0:T(8,128)}, f32[64,2048]{1,0:T(8,128)}, f32[4,256]{1,0:T(4,128)}) custom-call(f32[32,128]{1,0:T(8,128)S(1)} %get-tuple-element.9.best, f32[64,2048]{1,0:T(8,128)S(1)} %get-tuple-element.10.new, f32[4,256]{1,0:T(4,128)S(1)} %get-tuple-element.11.slot), custom_call_target="tpu_custom_call" | custom-call | tf_op jit(solution)/shard_map/hand_over/pallas_call | solution.py:445

commit v5 on v4

--- a/solution.py
+++ b/solution.py
@@ -117,7 +117,7 @@
 
             return 0
 
-        lax.fori_loop(0, n_dp, step, 0)
+        lax.fori_loop(0, n_dp, step, 0, unroll=2)
         recv[t, me] = sb[t, me]
 
     send_round(0)
@@ -330,6 +330,8 @@
         slot_out[pl.ds(t, 1), :] = jnp.where(m > -jnp.inf, m * irow, -1.0)
         return 0
 
+    lax.fori_loop(0, 4, block, 0)
+
     def got_sq(k, _):
         s = peer(k)
         sq_copy(s, s).wait_recv()
@@ -354,7 +356,6 @@
         top = jnp.maximum(top, rbest[s])
     best_out[...] = top
 
-    lax.fori_loop(0, 4, block, 0)
 
     def sent(k, _):
         p = peer(k)

time: 56.4 us -> 53.5 us (0.949)
  Pallas kernels: 55.7 us -> 52.7 us
    pallas_call x1, Pallas kernels: 54.8 us -> 51.9 us  [shards(): pl.pallas_call(body, out_shape=(jax.ShapeDtypeStruct((rows // 128, 128),...]
where the time goes in v5:
time: 53.5 us; the launch traced here: 53.4 us
  Pallas kernels  52.7 us (99%)
  between operations  0.64 us (1%)
    pallas_call x1, Pallas kernels, shards(): pl.pallas_call(body, out_shape=(jax.ShapeDtypeStruct((rows // 128, 128),...  51.9 us

profile of v5, /device:TPU:1, one launch (start us, length us, event | category | flops | bytes accessed | tf_op | source)
XLA Modules:
  0.0 53.4 jit_solution(17986085790545511847)
XLA Ops:
  0.6 51.9 %window.1 = (f32[32,128]{1,0:T(8,128)S(1)}, f32[64,2048]{1,0:T(8,128)S(1)}, f32[4,256]{1,0:T(4,128)S(1)}) custom-call(s32[8,4,16]{2,1,0:T(4,128)} %bitcast.9, s32[16,512]{1,0:T(8,128)} %bitcast.8, s32[512]{0:T(512)} %bitcast.11, s32[32,128]{1,0:T(8,128)} %bitcast.10, bf16[4096,1024]{1,0:T(8,128)(2,1)} %emb_hbm.1, bf16[2048,1024]{1,0:T(8,128)(2,1)} %cent_hbm.1), custom_call_target="tpu_custom_call" | custom-call | tf_op jit(solution)/shard_map/window/pallas_call | solution.py:390
  52.6 0.8 %hand_over.1 = (f32[32,128]{1,0:T(8,128)}, f32[64,2048]{1,0:T(8,128)}, f32[4,256]{1,0:T(4,128)}) custom-call(f32[32,128]{1,0:T(8,128)S(1)} %get-tuple-element.9.best, f32[64,2048]{1,0:T(8,128)S(1)} %get-tuple-element.10.new, f32[4,256]{1,0:T(4,128)S(1)} %get-tuple-element.11.slot), custom_call_target="tpu_custom_call" | custom-call | tf_op jit(solution)/shard_map/hand_over/pallas_call | solution.py:446

commit v6 on v5

--- a/solution.py
+++ b/solution.py
@@ -31,13 +31,14 @@
     me = lax.axis_index("dp")
     jc = lax.axis_index("cent")
     mx, my = me // 4, lax.rem(me, 4)
-    chunk = rows // 8
+    chunk = rows // 4
     share = pick.shape[1]
     cshard = cen.shape[0]
     lo_n = acc.shape[1]
     fpart = feat // n_dp
 
-    def peer(k):
+    def peer(i):
+        k = lax.rem(i * 7, 16)
         return lax.rem(mx + k // 4, 4) * 4 + lax.rem(my + lax.rem(k, 4), 4)
 
     def cpeer(k):
@@ -57,7 +58,7 @@
     ]
     for c in tables:
         c.start()
-    for i in range(8):
+    for i in range(4):
         load(i).start()
 
     barrier = pltpu.get_barrier_semaphore()
@@ -84,7 +85,7 @@
         lax.fori_loop(0, chunk // 16, widen, 0, unroll=4)
         return 0
 
-    lax.fori_loop(0, 8, widen_chunk, 0)
+    lax.fori_loop(0, 4, widen_chunk, 0)
     cent_load.start()
     for c in tables:
         c.wait()

time: 53.5 us -> 53.2 us (level)
  no operation moved by 1% of the time
where the time goes in v6:
time: 53.2 us; the launch traced here: 53.1 us
  Pallas kernels  52.4 us (98%)
  between operations  0.64 us (1%)
    pallas_call x1, Pallas kernels, shards(): pl.pallas_call(body, out_shape=(jax.ShapeDtypeStruct((rows // 128, 128),...  51.6 us

profile of v6, /device:TPU:1, one launch (start us, length us, event | category | flops | bytes accessed | tf_op | source)
XLA Modules:
  0.0 53.1 jit_solution(14710099180265472125)
XLA Ops:
  0.6 51.6 %window.1 = (f32[32,128]{1,0:T(8,128)S(1)}, f32[64,2048]{1,0:T(8,128)S(1)}, f32[4,256]{1,0:T(4,128)S(1)}) custom-call(s32[8,4,16]{2,1,0:T(4,128)} %bitcast.9, s32[16,512]{1,0:T(8,128)} %bitcast.8, s32[512]{0:T(512)} %bitcast.11, s32[32,128]{1,0:T(8,128)} %bitcast.10, bf16[4096,1024]{1,0:T(8,128)(2,1)} %emb_hbm.1, bf16[2048,1024]{1,0:T(8,128)(2,1)} %cent_hbm.1), custom_call_target="tpu_custom_call" | custom-call | tf_op jit(solution)/shard_map/window/pallas_call | solution.py:391
  52.2 0.8 %hand_over.1 = (f32[32,128]{1,0:T(8,128)}, f32[64,2048]{1,0:T(8,128)}, f32[4,256]{1,0:T(4,128)}) custom-call(f32[32,128]{1,0:T(8,128)S(1)} %get-tuple-element.9.best, f32[64,2048]{1,0:T(8,128)S(1)} %get-tuple-element.10.new, f32[4,256]{1,0:T(4,128)S(1)} %get-tuple-element.11.slot), custom_call_target="tpu_custom_call" | custom-call | tf_op jit(solution)/shard_map/hand_over/pallas_call | solution.py:447

commit v7 on v6

--- a/solution.py
+++ b/solution.py
@@ -184,12 +184,12 @@
     to_smem.wait()
 
     def take(n, _):
-        for u in range(16):
-            p = n * 16 + u
+        for u in range(32):
+            p = n * 32 + u
             xc[pl.ds(pl.multiple_of(p * 8, 8), 8), :] = slabs[jnp.clip(pick[0, p], 0, rows - 1)]
         return 0
 
-    lax.fori_loop(0, share // 16, take, 0)
+    lax.fori_loop(0, share // 32, take, 0)
     part = jnp.zeros((share, 128), F32)
     for c in range(8):
         v = xc[pl.ds(c, share, stride=8), :]
@@ -276,21 +276,22 @@
         lax.fori_loop(1, n_dp, send_sq, 0)
 
     blk = tmax.shape[0]
+    wide = 2048
 
     def score(b, _):
         pl.when(b == rows // blk - 1)(sum_rows)
         r = pl.multiple_of(b * blk, blk)
 
         def tile(n, _):
-            k0 = pl.multiple_of(n * blk, blk)
-            s = dot(emb[pl.ds(r, blk), :], cen[pl.ds(k0, blk), :], NT)
+            k0 = pl.multiple_of(n * wide, wide)
+            s = dot(emb[pl.ds(r, blk), :], cen[pl.ds(k0, wide), :], NT)
             m = s[:, 0:128]
-            for c in range(1, blk // 128):
+            for c in range(1, wide // 128):
                 m = jnp.maximum(m, s[:, c * 128:(c + 1) * 128])
             tmax[...] = jnp.where(n == 0, m, jnp.maximum(tmax[...], m))
             return 0
 
-        lax.fori_loop(0, cshard // blk, tile, 0)
+        lax.fori_loop(0, cshard // wide, tile, 0)
         top = jnp.max(tmax[...].T, axis=0, keepdims=True)
         nrm = jnp.sqrt(jnp.sum(sqp[pl.ds(r, blk), :].T, axis=0, keepdims=True) + EPS)
         top = top / nrm
@@ -331,7 +332,7 @@
         slot_out[pl.ds(t, 1), :] = jnp.where(m > -jnp.inf, m * irow, -1.0)
         return 0
 
-    lax.fori_loop(0, 4, block, 0)
+    lax.fori_loop(0, 4, block, 0, unroll=True)
 
     def got_sq(k, _):
         s = peer(k)

time: 53.2 us -> 51.7 us (0.972)
  Pallas kernels: 52.4 us -> 50.9 us
    pallas_call x1, Pallas kernels: 51.6 us -> 50.1 us  [shards(): pl.pallas_call(body, out_shape=(jax.ShapeDtypeStruct((rows // 128, 128),...]
where the time goes in v7:
time: 51.7 us; the launch traced here: 51.6 us
  Pallas kernels  50.9 us (98%)
  between operations  0.64 us (1%)
    pallas_call x1, Pallas kernels, shards(): pl.pallas_call(body, out_shape=(jax.ShapeDtypeStruct((rows // 128, 128),...  50.1 us

profile of v7, /device:TPU:1, one launch (start us, length us, event | category | flops | bytes accessed | tf_op | source)
XLA Modules:
  0.0 51.6 jit_solution(11808102509126088277)
XLA Ops:
  0.6 50.1 %window.1 = (f32[32,128]{1,0:T(8,128)S(1)}, f32[64,2048]{1,0:T(8,128)S(1)}, f32[4,256]{1,0:T(4,128)S(1)}) custom-call(s32[8,4,16]{2,1,0:T(4,128)} %bitcast.9, s32[16,512]{1,0:T(8,128)} %bitcast.8, s32[512]{0:T(512)} %bitcast.11, s32[32,128]{1,0:T(8,128)} %bitcast.10, bf16[4096,1024]{1,0:T(8,128)(2,1)} %emb_hbm.1, bf16[2048,1024]{1,0:T(8,128)(2,1)} %cent_hbm.1), custom_call_target="tpu_custom_call" | custom-call | tf_op jit(solution)/shard_map/window/pallas_call | solution.py:392
  50.8 0.8 %hand_over.1 = (f32[32,128]{1,0:T(8,128)}, f32[64,2048]{1,0:T(8,128)}, f32[4,256]{1,0:T(4,128)}) custom-call(f32[32,128]{1,0:T(8,128)S(1)} %get-tuple-element.9.best, f32[64,2048]{1,0:T(8,128)S(1)} %get-tuple-element.10.new, f32[4,256]{1,0:T(4,128)S(1)} %get-tuple-element.11.slot), custom_call_target="tpu_custom_call" | custom-call | tf_op jit(solution)/shard_map/hand_over/pallas_call | solution.py:448
